TPU v7x, 32 devices: a whole 2x2x4 slice. The times are simulated.
32 devices in a mesh: rep: 2 (over y), fsdp: 4 (over z), seq: 4 (over x, core).
Axes of the slice: x: 2, y: 2, z: 4, core: 2. Of those that a mesh axis runs over, the one named last changes fastest.
Arguments:
- latents: bfloat16 [8, 1024, 1152], P(('rep', 'fsdp'), 'seq'), may hold values from -6 to 6
- cond: bfloat16 [8, 1152], P(('rep', 'fsdp')), may hold values from -6 to 6
- w_ada: bfloat16 [1152, 6912], P(('fsdp', 'seq')), may hold values from -0.25 to 0.25
- b_ada: bfloat16 [6912], P(('fsdp', 'seq')), may hold values from -3 to 3
- w_qkv: bfloat16 [1152, 3456], P(('fsdp', 'seq')), may hold values from -0.1875 to 0.1875
- b_qv: bfloat16 [2304], P(('fsdp', 'seq')), may hold values from -3 to 3
- w_out: bfloat16 [1152, 1152], P(('fsdp', 'seq')), may hold values from -1.5 to 1.5
- b_out: bfloat16 [1152], P(('fsdp', 'seq')), may hold values from -3 to 3
- w_one: bfloat16 [1152, 4608], P(('fsdp', 'seq')), may hold values from -0.1875 to 0.1875
- b_one: bfloat16 [4608], P(('fsdp', 'seq')), may hold values from -3 to 3
- w_two: bfloat16 [4608, 1152], P(('fsdp', 'seq')), may hold values from -0.09375 to 0.09375
- b_two: bfloat16 [1152], P(('fsdp', 'seq')), may hold values from -3 to 3
- cotangent: bfloat16 [8, 1024, 1152], P(('rep', 'fsdp'), 'seq'), may hold values from -6 to 6
Outputs:
- block_out: bfloat16 [8, 1024, 1152], P(('rep', 'fsdp'), 'seq')
- grad_latents: float32 [8, 1024, 1152], P(('rep', 'fsdp'), 'seq')
- grad_cond: float32 [8, 1152], P(('rep', 'fsdp'))
- grad_w_ada: float32 [1152, 6912], P(('fsdp', 'seq'))
- grad_b_ada: float32 [6912], P(('fsdp', 'seq'))
- grad_w_qkv: float32 [1152, 3456], P(('fsdp', 'seq'))
- grad_b_qv: float32 [2304], P(('fsdp', 'seq'))
- grad_w_out: float32 [1152, 1152], P(('fsdp', 'seq'))
- grad_b_out: float32 [1152], P(('fsdp', 'seq'))
- grad_w_one: float32 [1152, 4608], P(('fsdp', 'seq'))
- grad_b_one: float32 [4608], P(('fsdp', 'seq'))
- grad_w_two: float32 [4608, 1152], P(('fsdp', 'seq'))
- grad_b_two: float32 [1152], P(('fsdp', 'seq'))
All inputs are finite; a program needn't handle non-finite values.
Results may differ from a plain program's by a relative error of at most 0.014.
The roundings to bfloat16 on the way count: a program that leaves them out, or rounds other values in their place, can miss the bound.
Values may be sent and summed in bfloat16 or wider, within the bound.
A program may use at most 448 MiB of HBM per device.

v0:
```python
import math
import jax
import jax.numpy as jnp
from jax import lax
from jax.sharding import PartitionSpec as P

H = 16
epsilon = 1e-06
gelu_coef = math.sqrt(2.0 / math.pi)


def norm_stats(values):
    center = values - jnp.mean(values, axis=-1, keepdims=True)
    inv_std = lax.rsqrt(jnp.mean(center * center, axis=-1, keepdims=True) + epsilon)
    return (center * inv_std, inv_std)


def norm_back(grad, normed, inv_std):
    return inv_std * (
        grad
        - jnp.mean(grad, axis=-1, keepdims=True)
        - normed * jnp.mean(grad * normed, axis=-1, keepdims=True)
    )


def gelu_tanh(values):
    inner = gelu_coef * (values + 0.044715 * values * values * values)
    return 0.5 * values * (1.0 + jnp.tanh(inner))


def gelu_slope(values):
    inner = gelu_coef * (values + 0.044715 * values * values * values)
    tanh_val = jnp.tanh(inner)
    return 0.5 * (1.0 + tanh_val) + 0.5 * values * (1.0 - tanh_val * tanh_val) * gelu_coef * (
        1.0 + 3.0 * 0.044715 * values * values
    )


def row_dot(left, right):
    return jnp.dot(left, right, preferred_element_type=jnp.float32)


def back_dot(grad, weight):
    return lax.dot_general(
        grad, weight, (((1,), (1,)), ((), ())), preferred_element_type=jnp.float32
    )


def outer_dot(left, grad):
    return lax.dot_general(left, grad, (((0,), (0,)), ((), ())), preferred_element_type=jnp.float32)


def pack_rows(arrays, groups):
    return jnp.concatenate([array.reshape(groups, -1) for array in arrays], axis=1).reshape(-1)


def unpack_rows(flat, layouts, groups):
    pieces = []
    offset = 0
    for layout in layouts:
        amount = math.prod(layout) // groups
        piece = flat[offset : offset + amount].reshape((layout[0] // groups,) + tuple(layout[1:]))
        pieces.append(piece)
        offset = offset + amount
    return pieces


def split_blocks(array, block_len):
    shape = array.shape
    return jnp.moveaxis(
        array.reshape(shape[:2] + (shape[2] // block_len, block_len) + shape[3:]), 2, 0
    )


def join_blocks(array):
    moved = jnp.moveaxis(array, 0, 2)
    shape = moved.shape
    return moved.reshape(shape[:2] + (shape[2] * shape[3],) + shape[4:])


def attention_forward(queries, key_rows, val_rows):
    length = queries.shape[2]
    head_size = queries.shape[3]
    block_len = min(512, length)
    score_scale = head_size ** (-0.5)

    def one_block(query_block):
        scores = (
            jnp.einsum("bhqd,bhkd->bhqk", query_block, key_rows, preferred_element_type=jnp.float32)
            * score_scale
        )
        highest = jnp.max(scores, axis=-1, keepdims=True)
        raised = jnp.exp(scores - highest)
        summed = jnp.sum(raised, axis=-1, keepdims=True)
        probs_low = (raised / summed).astype(jnp.bfloat16)
        result = jnp.einsum(
            "bhqk,bhkd->bhqd", probs_low, val_rows, preferred_element_type=jnp.float32
        )
        return (result.astype(jnp.bfloat16), (highest + jnp.log(summed))[..., 0])

    outputs, log_totals = lax.map(one_block, split_blocks(queries, block_len))
    return (join_blocks(outputs), join_blocks(log_totals))


def attention_backward(queries, key_rows, val_rows, log_totals, grad_out):
    length = queries.shape[2]
    head_size = queries.shape[3]
    block_len = min(512, length)
    score_scale = head_size ** (-0.5)

    def one_block(carried, pieces):
        grad_keys, grad_vals = carried
        query_block, grad_block, lse_block = pieces
        scores = (
            jnp.einsum("bhqd,bhkd->bhqk", query_block, key_rows, preferred_element_type=jnp.float32)
            * score_scale
        )
        attn_probs = jnp.exp(scores - lse_block[..., None])
        grad_probs = jnp.einsum(
            "bhqd,bhkd->bhqk", grad_block, val_rows, preferred_element_type=jnp.float32
        )
        row_inner = jnp.sum(attn_probs * grad_probs, axis=-1, keepdims=True)
        grad_scores = (attn_probs * (grad_probs - row_inner)).astype(jnp.bfloat16)
        grad_query = (
            jnp.einsum("bhqk,bhkd->bhqd", grad_scores, key_rows, preferred_element_type=jnp.float32)
            * score_scale
        )
        grad_keys = (
            grad_keys
            + jnp.einsum(
                "bhqk,bhqd->bhkd", grad_scores, query_block, preferred_element_type=jnp.float32
            )
            * score_scale
        )
        grad_vals = grad_vals + jnp.einsum(
            "bhqk,bhqd->bhkd",
            attn_probs.astype(jnp.bfloat16),
            grad_block,
            preferred_element_type=jnp.float32,
        )
        return ((grad_keys, grad_vals), grad_query)

    zeros_start = jnp.zeros(key_rows.shape, jnp.float32)
    pieces = (
        split_blocks(queries, block_len),
        split_blocks(grad_out, block_len),
        split_blocks(log_totals, block_len),
    )
    (grad_keys, grad_vals), grad_queries = lax.scan(one_block, (zeros_start, zeros_start), pieces)
    return (join_blocks(grad_queries), grad_keys, grad_vals)


def on_device(
    latents, cond, w_ada, b_ada, w_qkv, b_qv, w_out, b_out, w_one, b_one, w_two, b_two, cotangent
):
    latent_count, local_len, width = latents.shape
    token_rows = latent_count * local_len
    head_count = H
    head_size = width // head_count
    seq_count = lax.axis_size("seq")
    group_size = lax.axis_size(("fsdp", "seq"))
    local_heads = head_count // seq_count
    full_len = local_len * seq_count
    owner = lax.axis_index(("fsdp", "seq"))
    own_rows = w_ada.shape[0]
    bias_cols = b_ada.shape[0]
    first_latent = lax.axis_index(("rep", "fsdp")) * latent_count
    cond_float = cond.astype(jnp.float32)
    cond_sigmoid = jax.nn.sigmoid(cond_float)
    silu_cond = (cond_float * cond_sigmoid).astype(jnp.bfloat16)
    silu_every = lax.all_gather(silu_cond, ("rep", "fsdp"), axis=0, tiled=True)
    silu_owned = lax.dynamic_slice_in_dim(silu_every, owner * own_rows, own_rows, 1)
    ada_part = row_dot(silu_owned, w_ada)
    bias_slot = (
        lax.dynamic_slice_in_dim(ada_part, owner * bias_cols, bias_cols, 1)
        + b_ada.astype(jnp.float32)[None, :]
    )
    ada_part = lax.dynamic_update_slice_in_dim(ada_part, bias_slot, owner * bias_cols, 1)
    modulation_every = lax.psum(ada_part, ("fsdp", "seq"))
    modulation = lax.dynamic_slice_in_dim(modulation_every, first_latent, latent_count, 0)
    shift_one, scale_one, gate_one, shift_two, scale_two, gate_two = jnp.split(
        modulation[:, None, :], 6, axis=2
    )
    full_fwd = (
        lax.all_gather(w_qkv, ("fsdp", "seq"), axis=0, tiled=True),
        lax.all_gather(b_qv, ("fsdp", "seq"), axis=0, tiled=True),
        lax.all_gather(w_out, ("fsdp", "seq"), axis=0, tiled=True),
        lax.all_gather(b_out, ("fsdp", "seq"), axis=0, tiled=True),
        lax.all_gather(w_one, ("fsdp", "seq"), axis=0, tiled=True),
        lax.all_gather(b_one, ("fsdp", "seq"), axis=0, tiled=True),
        lax.all_gather(w_two, ("fsdp", "seq"), axis=0, tiled=True),
        lax.all_gather(b_two, ("fsdp", "seq"), axis=0, tiled=True),
    )
    qkv_full, qv_bias, out_full, out_bias, one_full, one_bias, two_full, two_bias = full_fwd
    inputs = latents.astype(jnp.float32)
    normed_one, inv_one = norm_stats(inputs)
    mixed_one = (
        (normed_one * (1.0 + scale_one) + shift_one).astype(jnp.bfloat16).reshape(token_rows, width)
    )
    bias_full = jnp.concatenate(
        [qv_bias[:width], jnp.zeros((width,), jnp.bfloat16), qv_bias[width:]]
    ).astype(jnp.float32)
    projected = (row_dot(mixed_one, qkv_full) + bias_full).astype(jnp.bfloat16)
    token_heads = projected.reshape(latent_count, local_len, 3, head_count, head_size).transpose(
        2, 0, 3, 1, 4
    )
    token_heads = token_heads.reshape(3, latent_count, head_count, local_len * head_size)
    head_tokens = lax.all_to_all(token_heads, "seq", split_axis=2, concat_axis=3, tiled=True)
    head_tokens = head_tokens.reshape(3, latent_count, local_heads, full_len, head_size)
    queries = head_tokens[0]
    key_rows = head_tokens[1]
    val_rows = head_tokens[2]
    attended, log_totals = attention_forward(queries, key_rows, val_rows)
    back_tokens = lax.all_to_all(
        attended.reshape(latent_count, local_heads, full_len * head_size),
        "seq",
        split_axis=2,
        concat_axis=1,
        tiled=True,
    )
    merged = (
        back_tokens.reshape(latent_count, head_count, local_len, head_size)
        .transpose(0, 2, 1, 3)
        .reshape(token_rows, width)
    )
    branch_one = (row_dot(merged, out_full) + out_bias.astype(jnp.float32)).reshape(
        latent_count, local_len, width
    )
    residual = inputs + gate_one * branch_one
    normed_two, inv_two = norm_stats(residual)
    mixed_two = (
        (normed_two * (1.0 + scale_two) + shift_two).astype(jnp.bfloat16).reshape(token_rows, width)
    )
    hidden_pre = row_dot(mixed_two, one_full) + one_bias.astype(jnp.float32)
    hidden_act = gelu_tanh(hidden_pre).astype(jnp.bfloat16)
    branch_two = (row_dot(hidden_act, two_full) + two_bias.astype(jnp.float32)).reshape(
        latent_count, local_len, width
    )
    block_out = (residual + gate_two * branch_two).astype(jnp.bfloat16)
    full_back = (
        lax.all_gather(w_qkv, ("fsdp", "seq"), axis=0, tiled=True),
        lax.all_gather(b_qv, ("fsdp", "seq"), axis=0, tiled=True),
        lax.all_gather(w_out, ("fsdp", "seq"), axis=0, tiled=True),
        lax.all_gather(b_out, ("fsdp", "seq"), axis=0, tiled=True),
        lax.all_gather(w_one, ("fsdp", "seq"), axis=0, tiled=True),
        lax.all_gather(b_one, ("fsdp", "seq"), axis=0, tiled=True),
        lax.all_gather(w_two, ("fsdp", "seq"), axis=0, tiled=True),
        lax.all_gather(b_two, ("fsdp", "seq"), axis=0, tiled=True),
    )
    qkv_back = full_back[0]
    out_back = full_back[2]
    one_back = full_back[4]
    two_back = full_back[6]
    grad_out = cotangent.astype(jnp.float32)
    grad_two = (gate_two * grad_out).astype(jnp.bfloat16).reshape(token_rows, width)
    gate_two_grad = jnp.sum(grad_out * branch_two, axis=1)
    two_w_grad = outer_dot(hidden_act, grad_two)
    two_b_grad = jnp.sum(grad_two, axis=0, dtype=jnp.float32)
    grad_pre = (back_dot(grad_two, two_back) * gelu_slope(hidden_pre)).astype(jnp.bfloat16)
    one_w_grad = outer_dot(mixed_two, grad_pre)
    one_b_grad = jnp.sum(grad_pre, axis=0, dtype=jnp.float32)
    grad_mixed_two = back_dot(grad_pre, one_back).reshape(latent_count, local_len, width)
    shift_two_grad = jnp.sum(grad_mixed_two, axis=1)
    scale_two_grad = jnp.sum(grad_mixed_two * normed_two, axis=1)
    grad_resid = grad_out + norm_back(grad_mixed_two * (1.0 + scale_two), normed_two, inv_two)
    mlp_layouts = (one_w_grad.shape, one_b_grad.shape, two_w_grad.shape, two_b_grad.shape)
    mlp_flat = lax.psum_scatter(
        pack_rows((one_w_grad, one_b_grad, two_w_grad, two_b_grad), group_size),
        ("fsdp", "seq"),
        scatter_dimension=0,
        tiled=True,
    )
    grad_branch = (gate_one * grad_resid).astype(jnp.bfloat16).reshape(token_rows, width)
    gate_one_grad = jnp.sum(grad_resid * branch_one, axis=1)
    out_w_grad = outer_dot(merged, grad_branch)
    out_b_grad = jnp.sum(grad_branch, axis=0, dtype=jnp.float32)
    grad_merged = back_dot(grad_branch, out_back).astype(jnp.bfloat16)
    grad_heads = grad_merged.reshape(latent_count, local_len, head_count, head_size).transpose(
        0, 2, 1, 3
    )
    grad_heads = grad_heads.reshape(latent_count, head_count, local_len * head_size)
    grad_heads = lax.all_to_all(grad_heads, "seq", split_axis=1, concat_axis=2, tiled=True)
    grad_heads = grad_heads.reshape(latent_count, local_heads, full_len, head_size)
    grad_queries, grad_keys, grad_vals = attention_backward(
        queries, key_rows, val_rows, log_totals, grad_heads
    )
    stacked = jnp.stack([grad_queries, grad_keys, grad_vals]).astype(jnp.bfloat16)
    stacked = stacked.reshape(3, latent_count, local_heads, full_len * head_size)
    grad_tokens = lax.all_to_all(stacked, "seq", split_axis=3, concat_axis=2, tiled=True)
    grad_proj = grad_tokens.reshape(3, latent_count, head_count, local_len, head_size).transpose(
        1, 3, 0, 2, 4
    )
    grad_proj = grad_proj.reshape(token_rows, 3 * width)
    qkv_w_grad = outer_dot(mixed_one, grad_proj)
    proj_sums = jnp.sum(grad_proj, axis=0, dtype=jnp.float32)
    qv_b_grad = jnp.concatenate([proj_sums[:width], proj_sums[2 * width :]])
    grad_mixed_one = back_dot(grad_proj, qkv_back).reshape(latent_count, local_len, width)
    shift_one_grad = jnp.sum(grad_mixed_one, axis=1)
    scale_one_grad = jnp.sum(grad_mixed_one * normed_one, axis=1)
    grad_inputs = grad_resid + norm_back(grad_mixed_one * (1.0 + scale_one), normed_one, inv_one)
    partial_mod = jnp.concatenate(
        [
            shift_one_grad,
            scale_one_grad,
            gate_one_grad,
            shift_two_grad,
            scale_two_grad,
            gate_two_grad,
        ],
        axis=1,
    )
    mod_grad = lax.psum(partial_mod, "seq").astype(jnp.bfloat16)
    mod_every = lax.all_gather(mod_grad, ("rep", "fsdp"), axis=0, tiled=True)
    ada_w_grad = outer_dot(silu_owned, mod_every)
    ada_b_grad = jnp.sum(
        lax.dynamic_slice_in_dim(mod_every, owner * bias_cols, bias_cols, 1),
        axis=0,
        dtype=jnp.float32,
    )
    cond_part = back_dot(mod_every, w_ada)
    cond_every = lax.all_gather(cond_part, ("fsdp", "seq"), axis=1, tiled=True)
    cond_lin = lax.dynamic_slice_in_dim(cond_every, first_latent, latent_count, 0)
    cond_grad = cond_lin * cond_sigmoid * (1.0 + cond_float * (1.0 - cond_sigmoid))
    attn_layouts = (qkv_w_grad.shape, qv_b_grad.shape, out_w_grad.shape, out_b_grad.shape)
    attn_flat = lax.psum_scatter(
        pack_rows((qkv_w_grad, qv_b_grad, out_w_grad, out_b_grad), group_size),
        ("fsdp", "seq"),
        scatter_dimension=0,
        tiled=True,
    )
    attn_total, mlp_total = (
        lax.psum(attn_flat.astype(jnp.bfloat16), "rep").astype(jnp.float32),
        lax.psum(mlp_flat.astype(jnp.bfloat16), "rep").astype(jnp.float32),
    )
    attn_parts = unpack_rows(attn_total, attn_layouts, group_size)
    mlp_parts = unpack_rows(mlp_total, mlp_layouts, group_size)
    return (
        block_out,
        grad_inputs,
        cond_grad,
        ada_w_grad,
        ada_b_grad,
        attn_parts[0],
        attn_parts[1],
        attn_parts[2],
        attn_parts[3],
        mlp_parts[0],
        mlp_parts[1],
        mlp_parts[2],
        mlp_parts[3],
    )


def solution(mesh):
    in_specs = (
        P(("rep", "fsdp"), "seq", None),
        P(("rep", "fsdp"), None),
        P(("fsdp", "seq"), None),
        P(("fsdp", "seq")),
        P(("fsdp", "seq"), None),
        P(("fsdp", "seq")),
        P(("fsdp", "seq"), None),
        P(("fsdp", "seq")),
        P(("fsdp", "seq"), None),
        P(("fsdp", "seq")),
        P(("fsdp", "seq"), None),
        P(("fsdp", "seq")),
        P(("rep", "fsdp"), "seq", None),
    )
    out_specs = (
        P(("rep", "fsdp"), "seq", None),
        P(("rep", "fsdp"), "seq", None),
        P(("rep", "fsdp"), None),
        P(("fsdp", "seq"), None),
        P(("fsdp", "seq")),
        P(("fsdp", "seq"), None),
        P(("fsdp", "seq")),
        P(("fsdp", "seq"), None),
        P(("fsdp", "seq")),
        P(("fsdp", "seq"), None),
        P(("fsdp", "seq")),
        P(("fsdp", "seq"), None),
        P(("fsdp", "seq")),
    )
    return jax.shard_map(
        on_device, mesh=mesh, in_specs=in_specs, out_specs=out_specs, check_vma=False
    )
```

profile of v0, /device:TPU:0, one launch (start us, length us, event | category | flops | bytes accessed | tf_op | source)
XLA Modules:
  0.0 3231.1 jit_solution(2037017178745607638)
XLA Ops:
  8.7 32.3 %all-gather = bf16[8,1,1152]{2,1,0:T(2,128)(2,1)S(1)} all-gather(bf16[1,1,1152]{2,1,0:T(2,128)(2,1)S(1)} %get-tuple-element.247), channel_id=1, replica_groups=mesh['rep'=2,'fsdp'=4,'seq'=4] {'rep','fsdp'}, dimensions={0}, use_global_device_ids=true | all-gather | bytes 20736 | tf_op jit(solution)/shard_map/all_gather | solution.py:171
  50.0 57.8 %all-reduce.7 = (bf16[2304]{0:T(1024)(128)(2,1)S(1)}, bf16[1152]{0:T(1024)(128)(2,1)S(1)}, bf16[1152]{0:T(1024)(128)(2,1)S(1)}, bf16[4608]{0:T(1024)(128)(2,1)S(1)}) all-reduce(bf16[2304]{0:T(1024)(128)(2,1)S(1)} %dynamic-update-slice, bf16[1152]{0:T(1024)(128)(2,1)S(1)} %dynamic-update-slice.1, ...), channel_id=1, replica_groups=mesh['rep'=2,'fsdp'=4,'seq'=4] {'fsdp','seq'}, use_global_device_ids=true, to_apply=%add | all-reduce | flops 9216 | bytes 36864
  108.3 25.0 all-reduce.13.cloned.1.call-done
  134.9 73.7 %all-gather.8.cloned.1.call-done = bf16[1152,3456]{1,0:T(8,128)(2,1)} async-done(((bf16[72,3456]{1,0:T(8,128)(2,1)}), bf16[1152,3456]{1,0:T(8,128)(2,1)}) %all-gather.8.cloned.1.call-update) | async-done | bytes 7962640 | tf_op jit(solution)/shard_map/all_gather | solution.py:185
  208.7 7.2 fusion.46
  221.3 8.1 reshape.492
  233.5 35.5 %all-to-all-done = bf16[3,1,16,18432]{3,0,1,2:T(4,128)(2,1)S(1)} async-done(((bf16[3,1,16,18432]{3,0,1,2:T(4,128)(2,1)}), bf16[3,1,16,18432]{3,0,1,2:T(4,128)(2,1)S(1)}, u32[]{:S(2)}, u32[]{:S(2)}) %all-to-all-start) | async-done | bytes 1769504 | tf_op jit(solution)/shard_map/all_to_all | solution.py:208
  283.6 11.3 while.27
  299.4 56.5 %copy.113 = bf16[1,4,73728]{1,0,2:T(2,128)(2,1)} copy(bf16[1,4,73728]{2,1,0:T(4,128)(2,1)S(1)} %reshape_reshape.6) | data formatting | bytes 1179648 | tf_op jit(solution)/shard_map/reshape;reshape | solution.py:215
  356.5 400.0 %reduce.40 = bf16[73728,4]{1,0:T(8,128)(2,1)} reduce(bf16[73728,1,4]{2,1,0:T(2,128)(2,1)} %bitcast.242, bf16[]{:T(256)} %broadcast.232), dimensions={1}, to_apply=%bitcast.165.reduce_sub_computation | reduce | bytes 1179650
  756.5 51.0 %reshape.503 = bf16[4,2,36864]{2,1,0:T(2,128)(2,1)} reshape(bf16[73728,4]{1,0:T(8,128)(2,1)} %reduce.40) | data formatting | bytes 1179648
  807.5 4.6 all-to-all-start.1
  813.4 8.2 all-to-all-done.1
  821.7 61.7 %reshape.504 = bf16[73728,1,4]{2,1,0:T(2,128)(2,1)} reshape(bf16[4,2,36864]{2,1,0:T(2,128)(2,1)} %all-to-all-done.1) | data formatting | bytes 1179648
  883.4 69.2 %copy.114 = bf16[1,4,73728]{2,1,0:T(4,128)(2,1)} copy(bf16[1,4,73728]{1,0,2:T(2,128)(2,1)} %bitcast.243) | data formatting | bytes 1179648 | tf_op jit(solution)/shard_map/all_to_all | solution.py:214
  969.2 9.9 convolution_add_fusion
  979.1 8.2 convert_reduce_fusion.1
  987.3 9.1 fusion.92
  996.5 8.1 fusion.95
  1004.6 9.3 fusion.67
  1023.3 5.3 reshape.493
  1028.7 6.0 reduce.41
  1037.0 4.6 all-to-all-start.2
  1041.6 19.7 reshape.451
  1061.3 15.1 constant_dynamic-update-slice_fusion.7
  1089.0 5.5 bitcast_reduce_fusion
  1105.1 38.5 %while.28 = (s32[]{:T(128)}, f32[1,4,1024,72]{2,3,1,0:T(8,128)}, f32[1,4,1024,72]{2,3,1,0:T(8,128)S(1)}, bf16[2,1,4,512,72]{3,4,2,1,0:T(8,128)(2,1)}, bf16[2,1,4...) while((s32[]{:T(128)}, f32[1,4,1024,72]{2,3,1,0:T(8,128)}, ...), condition=%wide.region_13.14_spmd.clone, body=%wide.region_11.13_spmd.clone.sunk | while | flops 1536735232 | bytes 133357912 | solution.py:149
  1117.3 4.6 fusion.153
  1136.6 4.6 fusion.153
  1159.2 70.1 %copy.128 = bf16[3,1,4,73728]{2,0,1,3:T(4,128)(2,1)} copy(bf16[3,1,4,73728]{3,2,1,0:T(4,128)(2,1)S(1)} %pad_maximum_fusion) | data formatting | bytes 3538944 | tf_op jit(solution)/shard_map/stack | solution.py:287
  1229.2 89.9 %reshape.507 = bf16[4,2,110592]{2,1,0:T(2,128)(2,1)} reshape(bf16[73728,1,3,4]{3,2,1,0:T(4,128)(2,1)} %bitcast.169) | data formatting | bytes 3538944
  1322.9 13.6 fusion.77
  1336.6 19.7 reshape.453
  1357.8 57.9 %dynamic-update-slice.6 = f32[16,663912]{1,0:T(8,128)} dynamic-update-slice(f32[16,663912]{1,0:T(8,128)} %dynamic-update-slice.5, f32[16,331776]{1,0:T(8,128)} %reshape.453, s32[]{} %constant.143, s32[]{} %constant.145) | dynamic-update-slice | bytes 42467332
  1417.2 56.3 %reshape.455 = f32[10622592]{0:T(1024)} reshape(f32[16,663912]{1,0:T(8,128)} %dynamic-update-slice.7) | data formatting | bytes 84980736 | tf_op jit(solution)/shard_map/reshape | solution.py:54
  1473.5 102.3 %reshape.508 = bf16[73728,1,3,4]{3,2,1,0:T(4,128)(2,1)} reshape(bf16[4,2,110592]{2,1,0:T(2,128)(2,1)S(1)} %all-to-all-done.3) | data formatting | bytes 3538944
  1575.8 101.6 %copy.134 = bf16[3,1,4,4,18432]{4,3,2,0,1:T(4,128)(2,1)} copy(bf16[3,1,4,4,18432]{2,0,4,3,1:T(4,128)(2,1)} %bitcast.33) | data formatting | bytes 3538944 | tf_op jit(solution)/shard_map/all_to_all | solution.py:289
  1680.2 8.4 reshape.439
  1694.6 8.2 fusion.89
  1702.7 6.2 fusion.64
  1710.2 15.0 reshape.445
  1725.1 11.0 constant_dynamic-update-slice_fusion.6
  1737.6 16.0 dynamic-update-slice.10
  1755.2 26.6 reshape.448
  1781.8 1341.9 %all-reduce.16 = (bf16[5311872]{0:T(1024)(128)(2,1)}, bf16[10622592]{0:T(1024)(128)(2,1)}) all-reduce(f32[5311872]{0:T(1024)} %reshape.448, f32[10622592]{0:T(1024)} %reshape.455), channel_id=2, replica_groups=mesh['rep'=2,'fsdp'=4,'seq'=4] {'fsdp','seq'}, use_global_device_ids=true, to_apply=%region_26.27.clone | all-reduce | flops 15934464 | bytes 95606784
  3132.6 22.9 psum.29
  3155.6 31.3 all-gather.1
  3187.2 18.8 all-gather.2
  (284 shorter events, 193.8 us)
Async XLA Ops:
  7.2 35.2 %copy-start = (bf16[72,6912]{1,0:T(8,128)(2,1)S(1)}, bf16[72,6912]{1,0:T(8,128)(2,1)}, u32[]{:S(2)}) copy-start(bf16[72,6912]{1,0:T(8,128)(2,1)} %param.19) | copy-start | bytes 2985988
  7.2 39.2 %copy-start.51 = (u32[32]{0:T(128)S(1)}, u32[32]{0:T(128)}, u32[]{:S(2)}) copy-start(u32[32]{0:T(128)} %constant.104) | copy-start | bytes 388
  7.2 41.8 %copy-start.53 = (bf16[72]{0:T(256)(128)(2,1)S(1)}, bf16[72]{0:T(256)(128)(2,1)}, u32[]{:S(2)}) copy-start(bf16[72]{0:T(256)(128)(2,1)} %param.24) | copy-start | bytes 436
  7.2 42.0 %copy-start.54 = (bf16[72]{0:T(256)(128)(2,1)S(1)}, bf16[72]{0:T(256)(128)(2,1)}, u32[]{:S(2)}) copy-start(bf16[72]{0:T(256)(128)(2,1)} %param.28) | copy-start | bytes 436
  7.2 42.3 %copy-start.55 = (bf16[144]{0:T(256)(128)(2,1)S(1)}, bf16[144]{0:T(256)(128)(2,1)}, u32[]{:S(2)}) copy-start(bf16[144]{0:T(256)(128)(2,1)} %param.22) | copy-start | bytes 868
  7.2 42.5 %copy-start.52 = (bf16[288]{0:T(512)(128)(2,1)S(1)}, bf16[288]{0:T(512)(128)(2,1)}, u32[]{:S(2)}) copy-start(bf16[288]{0:T(512)(128)(2,1)} %param.26) | copy-start | bytes 1732
  7.2 100.5 %copy-start.10 = (bf16[1,256,1152]{2,1,0:T(8,128)(2,1)S(1)}, bf16[1,256,1152]{2,1,0:T(8,128)(2,1)}, u32[]{:S(2)}) copy-start(bf16[1,256,1152]{2,1,0:T(8,128)(2,1)} %param.17) | copy-start | bytes 1769476
  7.3 126.1 %all-reduce.13.cloned.1.call-start = ((), (), s32[]{:S(2)}) async-start(), calls=%async_computation.4 | async-start | bytes 442368 | tf_op jit(solution)/shard_map/psum | solution.py:179
  43.8 164.9 %all-gather.8.cloned.1.call-start = ((), (), s32[]{:S(2)}) async-start(), calls=%async_computation.5 | async-start | bytes 8460288 | tf_op jit(solution)/shard_map/all_gather | solution.py:185
  44.5 919.2 %all-gather.10.cloned.1.call-start = ((), (), s32[]{:S(2)}) async-start(), calls=%async_computation.6 | async-start | bytes 2820096 | tf_op jit(solution)/shard_map/all_gather | solution.py:187
  45.2 923.9 %all-gather.12.cloned.1.call-start = ((), (), s32[]{:S(2)}) async-start(), calls=%async_computation.7 | async-start | bytes 11280384 | tf_op jit(solution)/shard_map/all_gather | solution.py:189
  45.8 933.3 %all-gather.14.cloned.1.call-start = ((), (), s32[]{:S(2)}) async-start(), calls=%async_computation.8 | async-start | bytes 11280384 | tf_op jit(solution)/shard_map/all_gather | solution.py:191
  108.0 100.7 %copy-start.38 = (f32[256]{0:T(256)}, f32[256]{0:T(256)S(1)}, u32[]{:S(2)}) copy-start(f32[256]{0:T(256)S(1)} %broadcast_multiply_fusion.5) | copy-start | bytes 3076
  108.3 100.4 %copy-start.42 = (f32[256]{0:T(256)}, f32[256]{0:T(256)S(1)}, u32[]{:S(2)}) copy-start(f32[256]{0:T(256)S(1)} %add_rsqrt_fusion.1) | copy-start | bytes 3076
  134.9 73.7 %copy-start.27 = (f32[1152]{0:T(1024)}, f32[1152]{0:T(1024)S(1)}, u32[]{:S(2)}) copy-start(f32[1152]{0:T(1024)S(1)} %get-tuple-element.202) | copy-start | bytes 13828
  134.9 73.7 %copy-start.30 = (f32[1152]{0:T(1024)}, f32[1152]{0:T(1024)S(1)}, u32[]{:S(2)}) copy-start(f32[1152]{0:T(1024)S(1)} %get-tuple-element.201) | copy-start | bytes 13828
  229.4 39.6 %all-to-all-start = ((bf16[3,1,16,18432]{3,0,1,2:T(4,128)(2,1)}), bf16[3,1,16,18432]{3,0,1,2:T(4,128)(2,1)S(1)}, u32[]{:S(2)}, u32[]{:S(2)}) async-start(bf16[3,1,16,18432]{3,0,1,2:T(4,128)(2,1)} %reshape.492), calls=%async_computation | async-start | bytes 4718592 | tf_op jit(solution)/shard_map/all_to_all | solution.py:208
  278.0 5.6 copy-start.26
  294.9 61.0 %copy-start.4 = (bf16[1,4,1024,72]{2,3,1,0:T(8,128)(2,1)}, bf16[1,4,1024,72]{2,3,1,0:T(8,128)(2,1)S(1)}, u32[]{:S(2)}) copy-start(bf16[1,4,1024,72]{2,3,1,0:T(8,128)(2,1)S(1)} %get-tuple-element.443) | copy-start | bytes 1769476
  294.9 61.0 %copy-start.33 = (f32[2,1,4,512]{3,2,1,0:T(4,128)}, f32[2,1,4,512]{3,2,1,0:T(4,128)S(1)}, u32[]{:S(2)}) copy-start(f32[2,1,4,512]{3,2,1,0:T(4,128)S(1)} %get-tuple-element.405) | copy-start | bytes 49156
  807.5 14.2 all-to-all-start.1
  963.7 5.5 copy-start.29
  963.7 5.5 copy-start.32
  969.2 9.9 copy-start.36
  979.1 8.2 copy-start.9
  996.5 8.1 copy-start.14
  996.5 8.1 copy-start.18
  1037.0 48.5 %all-to-all-start.2 = ((bf16[4,2,36864]{2,1,0:T(2,128)(2,1)}), bf16[4,2,36864]{2,1,0:T(2,128)(2,1)}, u32[]{:S(2)}, u32[]{:S(2)}) async-start(bf16[4,2,36864]{2,1,0:T(2,128)(2,1)} %reshape.505), calls=%async_computation.2 | async-start | bytes 1179648 | tf_op jit(solution)/shard_map/all_to_all | solution.py:282
  1061.3 15.1 copy-start.12
  1061.3 15.1 copy-start.21
  1096.6 8.6 copy-start.34
  1113.1 4.2 copy-start.7
  1117.3 4.6 copy-start.2
  1117.3 4.8 copy-start.24
  1132.1 4.5 copy-start.7
  1136.6 4.6 copy-start.2
  1136.6 4.8 copy-start.24
  1143.6 5.1 copy-start.3
  1149.5 6.9 copy-start.22
  1319.1 154.4 %all-to-all-start.3 = ((bf16[4,2,110592]{2,1,0:T(2,128)(2,1)}), bf16[4,2,110592]{2,1,0:T(2,128)(2,1)S(1)}, u32[]{:S(2)}, u32[]{:S(2)}) async-start(bf16[4,2,110592]{2,1,0:T(2,128)(2,1)} %reshape.507), calls=%async_computation.3 | async-start | bytes 3538944 | tf_op jit(solution)/shard_map/all_to_all | solution.py:289
  1322.9 1886.3 %all-reduce.15.cloned.1.call-start = ((), (), s32[]{:S(2)}) async-start(), calls=%async_computation.9 | async-start | bytes 3989504 | tf_op jit(solution)/shard_map/psum | solution.py:332
  1336.5 19.7 copy-start.40
  1336.6 19.8 copy-start.35
  1737.6 16.0 copy-start.41
  3129.3 77.6 %copy-start.47 = (bf16[8,1,72]{2,1,0:T(2,128)(2,1)S(1)}, bf16[8,1,72]{2,1,0:T(2,128)(2,1)}, u32[]{:S(2)}) copy-start(bf16[8,1,72]{2,1,0:T(2,128)(2,1)} %copy-done.46) | copy-start | bytes 3460
  3132.5 76.1 %copy-start.44 = (bf16[1,1152]{1,0:T(2,128)(2,1)S(1)}, bf16[1,1152]{1,0:T(2,128)(2,1)}, u32[]{:S(2)}) copy-start(bf16[1,1152]{1,0:T(2,128)(2,1)} %param.18) | copy-start | bytes 6916
  3132.5 76.1 %copy-start.45 = (f32[1,1152]{1,0:T(1,128)S(1)}, f32[1,1152]{1,0:T(1,128)}, u32[]{:S(2)}) copy-start(f32[1,1152]{1,0:T(1,128)} %get-tuple-element.248) | copy-start | bytes 13828
  3209.2 5.5 copy-start.13
  (25 other events, 58.0 us)
Sparse Core Ops, SparseCore 0:
  43.9 89.4 all-reduce.12
  135.5 73.1 all-gather.7
  210.8 48.3 all-gather.9
  261.4 87.6 all-gather.11
  351.2 86.8 all-gather.13
  3129.4 68.6 all-reduce.14
where the time goes:
time: 3250 us; the launch traced here: 3230 us
  blocking collectives  1510 us (46%)
  local copies, waits for them, and re-layouts  984 us (30%)
  other arithmetic  434 us (13%)
  waiting for transfers between devices  145 us (4%)
  matrix products  128 us (4%)
    unnamed x2, blocking collectives  1400 us
    unnamed x127, local copies, waits for them, and re-layouts  428 us
    unnamed x5, other arithmetic  407 us
    all_to_all x2, local copies, waits for them, and re-layouts, on_device(): lax.all_to_all(stacked, 'seq', split_axis=3, concat_axis=2, tiled=True)  104 us
    reshape x2, local copies, waits for them, and re-layouts, pack_rows(): jnp.concatenate([array.reshape(groups, -1) for array in arrays], axis=1)  82.9 us
    another operation x4, local copies, waits for them, and re-layouts, on_device(): jnp.stack([grad_queries, grad_keys, grad_vals]).astype(jnp.bfloat16)  78 us
    all_to_all x3, local copies, waits for them, and re-layouts, on_device(): lax.all_to_all(attended.reshape(latent_count, local_heads, full_len * hea...  73.9 us
    all_gather x1, waiting for transfers between devices, on_device(): lax.all_gather(w_qkv, ('fsdp', 'seq'), axis=0, tiled=True)  73.7 us
  transfers between devices with their start and end apart: 10, of which 4 were waited for; matrix products, arithmetic and copies ran while one was open for 28% of the time, Pallas kernels for 0%

commit v1 on v0

--- a/solution.py
+++ b/solution.py
@@ -7,6 +7,29 @@
 H = 16
 epsilon = 1e-06
 gelu_coef = math.sqrt(2.0 / math.pi)
+
+
+def split_up(x, dim, length):
+    lengths = x.shape
+    tiles = x.reshape(*lengths[:dim], length, lengths[dim] // length, *lengths[dim + 1 :])
+    return jnp.moveaxis(tiles, dim, 0)
+
+
+def laid_out(tiles, dim):
+    tiles = jnp.moveaxis(tiles, 0, dim)
+    lengths = tiles.shape
+    return tiles.reshape(*lengths[:dim], lengths[dim] * lengths[dim + 1], *lengths[dim + 2 :])
+
+
+def swapped_with_each(shard, axis, split_dim, concat_dim):
+    count, here = (lax.axis_size(axis), lax.axis_index(axis))
+    parts = split_up(shard, split_dim, count)
+    outs = [parts[here]]
+    for hop in range(1, count):
+        sent = parts[here ^ hop]
+        outs.append(lax.ppermute(sent, axis, [(i, i ^ hop) for i in range(count)]))
+    parts = jnp.stack(outs)[here ^ jnp.arange(count)]
+    return laid_out(parts, concat_dim)
 
 
 def norm_stats(values):
@@ -286,7 +309,7 @@
     )
     stacked = jnp.stack([grad_queries, grad_keys, grad_vals]).astype(jnp.bfloat16)
     stacked = stacked.reshape(3, latent_count, local_heads, full_len * head_size)
-    grad_tokens = lax.all_to_all(stacked, "seq", split_axis=3, concat_axis=2, tiled=True)
+    grad_tokens = swapped_with_each(stacked, "seq", 3, 2)
     grad_proj = grad_tokens.reshape(3, latent_count, head_count, local_len, head_size).transpose(
         1, 3, 0, 2, 4
     )

time: 3250 us -> 2890 us (0.89)
  local copies, waits for them, and re-layouts: 984 us -> 640 us
    unnamed x127 -> x137, local copies, waits for them, and re-layouts: 428 us -> 242 us
    all_to_all x2 -> x0, local copies, waits for them, and re-layouts: 104 us -> none  [on_device(): lax.all_to_all(stacked, 'seq', split_axis=3, concat_axis=2, tiled=True)]
    another operation x4, local copies, waits for them, and re-layouts: 78 us -> 11.9 us  [on_device(): jnp.stack([grad_queries, grad_keys, grad_vals]).astype(jnp.bfloat16)]
    unnamed x5 -> x6, other arithmetic: 407 us -> 407 us
  transfers between devices with their start and end apart: 10 -> 12, of which waited for: 4 -> 4; matrix products, arithmetic and copies ran while one was open for 28% -> 32% of each run, Pallas kernels for 0% -> 0%
where the time goes in v1:
time: 2890 us; the launch traced here: 2880 us
  blocking collectives  1500 us (52%)
  local copies, waits for them, and re-layouts  640 us (22%)
  other arithmetic  435 us (15%)
  waiting for transfers between devices  144 us (5%)
  matrix products  124 us (4%)
    unnamed x2, blocking collectives  1390 us
    unnamed x6, other arithmetic  407 us
    unnamed x137, local copies, waits for them, and re-layouts  242 us
    reshape x2, local copies, waits for them, and re-layouts, pack_rows(): jnp.concatenate([array.reshape(groups, -1) for array in arrays], axis=1)  82.8 us
    all_to_all x3, local copies, waits for them, and re-layouts, on_device(): lax.all_to_all(attended.reshape(latent_count, local_heads, full_len * hea...  73.9 us
    all_gather x1, waiting for transfers between devices, on_device(): lax.all_gather(w_qkv, ('fsdp', 'seq'), axis=0, tiled=True)  73.7 us
    reshape x7, local copies, waits for them, and re-layouts, pack_rows(): array.reshape(groups, -1)  59.6 us
    another operation x2, local copies, waits for them, and re-layouts, on_device(): attended.reshape(latent_count, local_heads, full_len * head_size)  59.5 us
  transfers between devices with their start and end apart: 12, of which 4 were waited for; matrix products, arithmetic and copies ran while one was open for 32% of the time, Pallas kernels for 0%

profile of v1, /device:TPU:0, one launch (start us, length us, event | category | flops | bytes accessed | tf_op | source)
XLA Modules:
  0.0 2876.9 jit_solution(3698009586870991052)
XLA Ops:
  8.6 32.3 %all-gather = bf16[8,1,1152]{2,1,0:T(2,128)(2,1)S(1)} all-gather(bf16[1,1,1152]{2,1,0:T(2,128)(2,1)S(1)} %get-tuple-element.232), channel_id=1, replica_groups=mesh['rep'=2,'fsdp'=4,'seq'=4] {'rep','fsdp'}, dimensions={0}, use_global_device_ids=true | all-gather | bytes 20736 | tf_op jit(solution)/shard_map/all_gather | solution.py:194
  50.0 57.8 %all-reduce.7 = (bf16[2304]{0:T(1024)(128)(2,1)S(1)}, bf16[1152]{0:T(1024)(128)(2,1)S(1)}, bf16[1152]{0:T(1024)(128)(2,1)S(1)}, bf16[4608]{0:T(1024)(128)(2,1)S(1)}) all-reduce(bf16[2304]{0:T(1024)(128)(2,1)S(1)} %dynamic-update-slice, bf16[1152]{0:T(1024)(128)(2,1)S(1)} %dynamic-update-slice.1, ...), channel_id=1, replica_groups=mesh['rep'=2,'fsdp'=4,'seq'=4] {'fsdp','seq'}, use_global_device_ids=true, to_apply=%add | all-reduce | flops 9216 | bytes 36864
  108.2 25.0 all-reduce.13.cloned.1.call-done
  134.9 73.7 %all-gather.8.cloned.1.call-done = bf16[1152,3456]{1,0:T(8,128)(2,1)} async-done(((bf16[72,3456]{1,0:T(8,128)(2,1)}), bf16[1152,3456]{1,0:T(8,128)(2,1)}) %all-gather.8.cloned.1.call-update) | async-done | bytes 7962640 | tf_op jit(solution)/shard_map/all_gather | solution.py:208
  208.6 7.2 fusion.46
  221.3 8.1 reshape.519
  233.5 35.5 %all-to-all-done = bf16[3,1,16,18432]{3,0,1,2:T(4,128)(2,1)S(1)} async-done(((bf16[3,1,16,18432]{3,0,1,2:T(4,128)(2,1)}), bf16[3,1,16,18432]{3,0,1,2:T(4,128)(2,1)S(1)}, u32[]{:S(2)}, u32[]{:S(2)}) %all-to-all-start) | async-done | bytes 1769504 | tf_op jit(solution)/shard_map/all_to_all | solution.py:231
  283.6 11.3 while.27
  299.4 56.5 %copy.83 = bf16[1,4,73728]{1,0,2:T(2,128)(2,1)} copy(bf16[1,4,73728]{2,1,0:T(4,128)(2,1)S(1)} %reshape_reshape.10) | data formatting | bytes 1179648 | tf_op jit(solution)/shard_map/reshape;reshape | solution.py:238
  356.4 400.1 %reduce.40 = bf16[73728,4]{1,0:T(8,128)(2,1)} reduce(bf16[73728,1,4]{2,1,0:T(2,128)(2,1)} %bitcast.260, bf16[]{:T(256)} %broadcast.267), dimensions={1}, to_apply=%bitcast.181.reduce_sub_computation | reduce | bytes 1179650
  756.5 51.0 %reshape.530 = bf16[4,2,36864]{2,1,0:T(2,128)(2,1)} reshape(bf16[73728,4]{1,0:T(8,128)(2,1)} %reduce.40) | data formatting | bytes 1179648
  807.5 4.5 all-to-all-start.1
  814.1 7.6 all-to-all-done.1
  821.7 61.6 %reshape.531 = bf16[73728,1,4]{2,1,0:T(2,128)(2,1)} reshape(bf16[4,2,36864]{2,1,0:T(2,128)(2,1)} %all-to-all-done.1) | data formatting | bytes 1179648
  883.3 69.2 %copy.84 = bf16[1,4,73728]{2,1,0:T(4,128)(2,1)} copy(bf16[1,4,73728]{1,0,2:T(2,128)(2,1)} %bitcast.261) | data formatting | bytes 1179648 | tf_op jit(solution)/shard_map/all_to_all | solution.py:237
  963.6 4.2 fusion.99
  969.1 9.8 convolution_add_fusion
  978.9 8.8 convert_reduce_fusion.1
  987.8 9.1 fusion.93
  996.9 8.1 fusion.96
  1005.0 9.3 fusion.67
  1023.7 5.3 reshape.520
  1029.0 6.0 reduce.41
  1041.5 20.1 reshape.468
  1061.7 14.9 constant_dynamic-update-slice_fusion.10
  1080.1 5.5 bitcast_reduce_fusion
  1096.2 38.7 %while.28 = (s32[]{:T(128)}, f32[1,4,1024,72]{2,3,1,0:T(8,128)}, f32[1,4,1024,72]{2,3,1,0:T(8,128)S(1)}, bf16[2,1,4,512,72]{3,4,2,1,0:T(8,128)(2,1)}, bf16[2,1,4...) while((s32[]{:T(128)}, f32[1,4,1024,72]{2,3,1,0:T(8,128)}, ...), condition=%wide.region_13.14_spmd.clone, body=%wide.region_11.13_spmd.clone.sunk | while | flops 1536735232 | bytes 133357912 | solution.py:172
  1104.2 4.2 fusion.153
  1108.4 4.6 fusion.154
  1123.3 4.5 fusion.153
  1127.8 4.6 fusion.154
  1157.1 4.5 constant_dynamic-slice_fusion.3
  1167.0 9.4 fusion.77
  1179.7 4.5 reshape.463
  1184.3 19.7 reshape.470
  1205.5 57.9 %dynamic-update-slice.6 = f32[16,663912]{1,0:T(8,128)} dynamic-update-slice(f32[16,663912]{1,0:T(8,128)} %dynamic-update-slice.5, f32[16,331776]{1,0:T(8,128)} %reshape.470, s32[]{} %constant.151, s32[]{} %constant.153) | dynamic-update-slice | bytes 42467332
  1265.2 56.2 %reshape.472 = f32[10622592]{0:T(1024)} reshape(f32[16,663912]{1,0:T(8,128)} %dynamic-update-slice.7) | data formatting | bytes 84980736 | tf_op jit(solution)/shard_map/reshape | solution.py:77
  1330.9 8.1 reshape_reshape.12
  1345.3 8.1 fusion.90
  1353.4 6.2 fusion.64
  1360.8 15.1 reshape.462
  1375.9 11.0 constant_dynamic-update-slice_fusion.9
  1388.5 16.0 dynamic-update-slice.10
  1406.0 26.6 reshape.465
  1432.6 1335.6 %all-reduce.16 = (bf16[5311872]{0:T(1024)(128)(2,1)}, bf16[10622592]{0:T(1024)(128)(2,1)}) all-reduce(f32[5311872]{0:T(1024)} %reshape.465, f32[10622592]{0:T(1024)} %reshape.472), channel_id=2, replica_groups=mesh['rep'=2,'fsdp'=4,'seq'=4] {'fsdp','seq'}, use_global_device_ids=true, to_apply=%region_26.27.clone | all-reduce | flops 15934464 | bytes 95606784
  2777.2 23.4 psum.29
  2800.5 31.2 %all-gather.1 = bf16[8,1,6912]{2,1,0:T(2,128)(2,1)S(1)} all-gather(bf16[1,1,6912]{2,1,0:T(2,128)(2,1)S(1)} %bitcast.286), channel_id=1, replica_groups=mesh['rep'=2,'fsdp'=4,'seq'=4] {'rep','fsdp'}, dimensions={0}, use_global_device_ids=true | all-gather | bytes 124416 | tf_op jit(solution)/shard_map/all_gather | solution.py:336
  2832.1 19.7 all-gather.2
  (302 shorter events, 195.9 us)
Async XLA Ops:
  7.2 35.1 %copy-start = (bf16[72,6912]{1,0:T(8,128)(2,1)S(1)}, bf16[72,6912]{1,0:T(8,128)(2,1)}, u32[]{:S(2)}) copy-start(bf16[72,6912]{1,0:T(8,128)(2,1)} %param.19) | copy-start | bytes 2985988
  7.2 126.1 %all-reduce.13.cloned.1.call-start = ((), (), s32[]{:S(2)}) async-start(), calls=%async_computation.3 | async-start | bytes 442368 | tf_op jit(solution)/shard_map/psum | solution.py:202
  42.3 6.6 copy-start.54
  42.3 6.9 copy-start.55
  42.3 7.1 copy-start.56
  42.3 7.4 copy-start.53
  42.3 65.4 %copy-start.10 = (bf16[1,256,1152]{2,1,0:T(8,128)(2,1)S(1)}, bf16[1,256,1152]{2,1,0:T(8,128)(2,1)}, u32[]{:S(2)}) copy-start(bf16[1,256,1152]{2,1,0:T(8,128)(2,1)} %param.17) | copy-start | bytes 1769476
  43.7 164.9 %all-gather.8.cloned.1.call-start = ((), (), s32[]{:S(2)}) async-start(), calls=%async_computation.4 | async-start | bytes 8460288 | tf_op jit(solution)/shard_map/all_gather | solution.py:208
  44.5 919.1 %all-gather.10.cloned.1.call-start = ((), (), s32[]{:S(2)}) async-start(), calls=%async_computation.5 | async-start | bytes 2820096 | tf_op jit(solution)/shard_map/all_gather | solution.py:210
  45.2 923.8 %all-gather.12.cloned.1.call-start = ((), (), s32[]{:S(2)}) async-start(), calls=%async_computation.6 | async-start | bytes 11280384 | tf_op jit(solution)/shard_map/all_gather | solution.py:212
  45.8 933.1 %all-gather.14.cloned.1.call-start = ((), (), s32[]{:S(2)}) async-start(), calls=%async_computation.7 | async-start | bytes 11280384 | tf_op jit(solution)/shard_map/all_gather | solution.py:214
  107.9 100.7 %copy-start.38 = (f32[256]{0:T(256)}, f32[256]{0:T(256)S(1)}, u32[]{:S(2)}) copy-start(f32[256]{0:T(256)S(1)} %broadcast_multiply_fusion.5) | copy-start | bytes 3076
  108.2 100.4 %copy-start.42 = (f32[256]{0:T(256)}, f32[256]{0:T(256)S(1)}, u32[]{:S(2)}) copy-start(f32[256]{0:T(256)S(1)} %add_rsqrt_fusion.1) | copy-start | bytes 3076
  134.9 73.7 %copy-start.31 = (f32[1152]{0:T(1024)}, f32[1152]{0:T(1024)S(1)}, u32[]{:S(2)}) copy-start(f32[1152]{0:T(1024)S(1)} %get-tuple-element.187) | copy-start | bytes 13828
  134.9 73.7 %copy-start.34 = (f32[1152]{0:T(1024)}, f32[1152]{0:T(1024)S(1)}, u32[]{:S(2)}) copy-start(f32[1152]{0:T(1024)S(1)} %get-tuple-element.186) | copy-start | bytes 13828
  229.4 39.6 %all-to-all-start = ((bf16[3,1,16,18432]{3,0,1,2:T(4,128)(2,1)}), bf16[3,1,16,18432]{3,0,1,2:T(4,128)(2,1)S(1)}, u32[]{:S(2)}, u32[]{:S(2)}) async-start(bf16[3,1,16,18432]{3,0,1,2:T(4,128)(2,1)} %reshape.519), calls=%async_computation | async-start | bytes 4718592 | tf_op jit(solution)/shard_map/all_to_all | solution.py:231
  278.0 5.6 copy-start.28
  294.9 61.0 %copy-start.4 = (bf16[1,4,1024,72]{2,3,1,0:T(8,128)(2,1)}, bf16[1,4,1024,72]{2,3,1,0:T(8,128)(2,1)S(1)}, u32[]{:S(2)}) copy-start(bf16[1,4,1024,72]{2,3,1,0:T(8,128)(2,1)S(1)} %get-tuple-element.432) | copy-start | bytes 1769476
  807.5 14.2 all-to-all-start.1
  963.5 5.5 copy-start.33
  963.6 5.5 copy-start.36
  969.1 9.9 copy-start.37
  978.9 8.8 copy-start.9
  996.9 8.1 copy-start.15
  996.9 8.1 copy-start.20
  1037.3 39.2 %all-to-all-start.2 = ((bf16[4,2,36864]{2,1,0:T(2,128)(2,1)}), bf16[4,2,36864]{2,1,0:T(2,128)(2,1)}, u32[]{:S(2)}, u32[]{:S(2)}) async-start(bf16[4,2,36864]{2,1,0:T(2,128)(2,1)} %reshape.532), calls=%async_computation.2 | async-start | bytes 1179648 | tf_op jit(solution)/shard_map/all_to_all | solution.py:305
  1041.5 1813.5 %all-reduce.15.cloned.1.call-start = ((), (), s32[]{:S(2)}) async-start(), calls=%async_computation.8 | async-start | bytes 3989504 | tf_op jit(solution)/shard_map/psum | solution.py:355
  1108.4 4.6 copy-start.2
  1108.4 4.8 copy-start.26
  1127.8 4.6 copy-start.2
  1127.8 4.8 copy-start.26
  1137.1 6.0 copy-start.3
  1149.1 6.3 copy-start.12
  1149.1 6.3 copy-start.24
  1155.6 11.3 slice-start
  1157.1 9.9 slice-start.1
  1161.6 5.4 copy-start.21
  1162.7 159.1 %collective-permute-start.2 = (bf16[3,1,4,18432]{3,2,0,1:T(4,128)(2,1)}, bf16[3,1,4,18432]{3,2,0,1:T(4,128)(2,1)S(1)}, u32[]{:S(2)}, u32[]{:S(2)}) collective-permute-start(bf16[3,1,4,18432]{3,2,0,1:T(4,128)(2,1)} %bitcast.220), channel_id=1, source_target_pairs={{0,3},{1,2},{2,1},{3,0},{4,7},{5,6},{6,5},{7,4},{8,11},{9,10},{10,... | collective-permute-start | bytes 1327112 | tf_op jit(solution)/shard_map/ppermute | solution.py:30
  1165.5 156.3 %collective-permute-start.1 = (bf16[3,1,4,18432]{3,2,0,1:T(4,128)(2,1)}, bf16[3,1,4,18432]{3,2,0,1:T(4,128)(2,1)S(1)}, u32[]{:S(2)}, u32[]{:S(2)}) collective-permute-start(bf16[3,1,4,18432]{3,2,0,1:T(4,128)(2,1)} %bitcast.221), channel_id=1, source_target_pairs={{0,2},{1,3},{2,0},{3,1},{4,6},{5,7},{6,4},{7,5},{8,10},{9,11},{10,... | collective-permute-start | bytes 1327112 | tf_op jit(solution)/shard_map/ppermute | solution.py:30
  1167.0 9.4 copy-start.13
  1167.0 9.4 copy-start.23
  1167.0 154.8 %collective-permute-start = (bf16[3,1,4,18432]{3,2,0,1:T(4,128)(2,1)}, bf16[3,1,4,18432]{3,2,0,1:T(4,128)(2,1)S(1)}, u32[]{:S(2)}, u32[]{:S(2)}) collective-permute-start(bf16[3,1,4,18432]{3,2,0,1:T(4,128)(2,1)} %bitcast.222), channel_id=1, source_target_pairs={{0,1},{1,0},{2,3},{3,2},{4,5},{5,4},{6,7},{7,6},{8,9},{9,8},{10,11... | collective-permute-start | bytes 1327112 | tf_op jit(solution)/shard_map/ppermute | solution.py:30
  1184.3 19.7 copy-start.40
  1265.2 56.2 %copy-start.18 = (bf16[3,1,4,1,18432]{4,3,2,1,0:T(2,128)(2,1)S(1)}, bf16[3,1,4,1,18432]{4,3,2,1,0:T(2,128)(2,1)}, u32[]{:S(2)}) copy-start(bf16[3,1,4,1,18432]{4,3,2,1,0:T(2,128)(2,1)} %get-tuple-element.238) | copy-start | bytes 1327108
  2777.0 75.6 %copy-start.48 = (bf16[8,1,72]{2,1,0:T(2,128)(2,1)S(1)}, bf16[8,1,72]{2,1,0:T(2,128)(2,1)}, u32[]{:S(2)}) copy-start(bf16[8,1,72]{2,1,0:T(2,128)(2,1)} %copy-done.47) | copy-start | bytes 3460
  2831.7 22.6 copy-start.45
  2831.7 22.6 copy-start.46
  2855.0 5.5 copy-start.14
  (30 other events, 76.0 us)
Sparse Core Ops, SparseCore 0:
  43.8 89.4 all-reduce.12
  135.5 73.1 all-gather.7
  210.8 48.3 all-gather.9
  261.3 87.6 all-gather.11
  351.2 86.8 all-gather.13
  2773.9 72.1 all-reduce.14
